TPU v7x, 32 devices: a whole 2x2x4 slice. The times are simulated.
32 devices in a mesh: groups: 2 (over y), ctx: 4 (over z), exp: 2 (over x), head: 2 (over core).
Axes of the slice: x: 2, y: 2, z: 4, core: 2. Of those that a mesh axis runs over, the one named last changes fastest.
Arguments:
- latent: bfloat16 [256, 576], P(('groups', 'ctx')), parts along dimension 0, may hold values from -5 to 5
- query: bfloat16 [256, 3072], P(('groups', 'ctx'), ('exp', 'head')), parts along dimension 0, may hold values from -30 to 30
- w_uk: bfloat16 [512, 2048], P(None, ('exp', 'head')), may hold values from -0.25 to 0.25
- w_uv: bfloat16 [512, 2048], P(None, ('exp', 'head')), may hold values from -0.25 to 0.25
- w_o: bfloat16 [2048, 3584], P(('exp', 'head'), 'ctx'), may hold values from -0.5 to 0.5
- resid: bfloat16 [256, 3584], P(('groups', 'ctx', 'exp', 'head')), parts along dimension 0, may hold values from -6 to 6
- norm_gain: float32 [3584], replicated, may hold values from 0.1 to 1.9
- w_gate: bfloat16 [4, 3584, 2048], P(('exp', 'head'), None, 'ctx'), may hold values from -0.09375 to 0.09375
- w_up: bfloat16 [4, 3584, 2048], P(('exp', 'head'), None, 'ctx'), may hold values from -0.09375 to 0.09375
- w_down: bfloat16 [4, 2048, 3584], P(('exp', 'head'), None, 'ctx'), may hold values from -0.125 to 0.125
- expert_ids: int32 [256, 2], P(('groups', 'ctx', 'exp', 'head')), parts along dimension 0, may hold values from 0 to 3, all different within a row; in each aligned block of 8 rows (0 to 7, 8 to 15, ...) at most 8 rows name the same one
- route_weights: float32 [256, 2], P(('groups', 'ctx', 'exp', 'head')), parts along dimension 0, may hold values from 0.2 to 1
Outputs:
- layer_out: bfloat16 [256, 3584], P(('groups', 'ctx', 'exp', 'head')), parts along dimension 0
There are 2 independent parts, one for each index of `groups`. A program takes and returns all parts, laid end to end along the dimension named above; an argument that names none is the same for every part. Nothing has to cross between parts.
Inputs may be any that keep to these rules, and one draw needn't show every extreme that they name: `expert_ids`: each token names 2 different experts; within each aligned block of 8 tokens no expert is named more than 8 times, a bound that some block reaches.
All inputs are finite; a program needn't handle non-finite values.
Results may differ from a plain program's by a relative error of at most 0.014.
Values may be sent and summed in bfloat16 or wider, within the bound.
A program may use at most 64 MiB of HBM per device.

v0:
```python
import math
import jax
import jax.numpy as jnp
from jax import lax
from jax.sharding import PartitionSpec as P

D = 3584
NOPE = 128
ROPE = 64
LATENT = 512


def shards(
    latent,
    query,
    w_uk,
    w_uv,
    w_o,
    resid,
    norm_gain,
    w_gate,
    w_up,
    w_down,
    expert_ids,
    route_weights,
):
    qblock = query.shape[0]
    head_width = NOPE + ROPE
    heads_here = query.shape[1] // head_width
    nope_span = heads_here * NOPE
    score_scale = 1.0 / math.sqrt(head_width)
    query_all = query.reshape(qblock, heads_here, head_width)
    query_nope = query_all[:, :, :NOPE]
    query_rope = query_all[:, :, NOPE:]
    query_pos = lax.axis_index("ctx") * qblock + jnp.arange(qblock, dtype=jnp.int32)
    shard_rows = lax.all_gather(latent, "ctx", axis=0, tiled=True)
    piece_rows = shard_rows.shape[0]
    compressed = shard_rows[:, :LATENT]
    key_nope = (
        jnp.dot(compressed, w_uk, preferred_element_type=jnp.float32)
        .astype(jnp.bfloat16)
        .reshape(piece_rows, heads_here, NOPE)
    )
    values = (
        jnp.dot(compressed, w_uv, preferred_element_type=jnp.float32)
        .astype(jnp.bfloat16)
        .reshape(piece_rows, heads_here, NOPE)
    )
    run_max = jnp.full((qblock, heads_here), -1e30, jnp.float32)
    piece_rows = key_nope.shape[0]
    scores = jnp.einsum("qhd,khd->qhk", query_nope, key_nope, preferred_element_type=jnp.float32)
    scores = (
        scores
        + jnp.einsum(
            "qhd,kd->qhk", query_rope, shard_rows[:, LATENT:], preferred_element_type=jnp.float32
        )
    ) * score_scale
    key_pos = jnp.arange(piece_rows, dtype=jnp.int32)
    allowed = (key_pos[None, :] <= query_pos[:, None])[:, None, :]
    new_max = jnp.maximum(run_max, jnp.max(jnp.where(allowed, scores, -1e30), axis=2))
    exponent = jnp.where(allowed, jnp.exp(scores - new_max[:, :, None]), 0.0)
    run_sum = jnp.sum(exponent, axis=2)
    weighted_sum = jnp.einsum(
        "qhk,khd->qhd", exponent.astype(jnp.bfloat16), values, preferred_element_type=jnp.float32
    )
    attn_state = (new_max, run_sum, weighted_sum)
    run_max, run_sum, weighted_sum = attn_state
    attended = (weighted_sum / run_sum[:, :, None]).astype(jnp.bfloat16).reshape(qblock, nope_span)
    tok_dev = resid.shape[0]
    ctx_count = lax.axis_size("ctx")
    partial_value = jnp.dot(
        lax.all_gather(attended, "ctx", axis=0, tiled=True), w_o, preferred_element_type=jnp.float32
    )
    partial_value = partial_value.astype(jnp.bfloat16).reshape(ctx_count, qblock, w_o.shape[1])
    summed = lax.psum_scatter(
        partial_value, ("exp", "head"), scatter_dimension=1, tiled=True
    ).astype(jnp.float32)
    swapped = lax.all_to_all(
        summed.astype(jnp.bfloat16), "ctx", split_axis=0, concat_axis=2, tiled=True
    ).astype(summed.dtype)
    projected = swapped.reshape(tok_dev, D)
    residual_sum = resid.astype(jnp.float32) + projected
    inverse_rms = lax.rsqrt(jnp.mean(residual_sum * residual_sum, axis=1, keepdims=True) + 1e-06)
    normalized = (residual_sum * inverse_rms * norm_gain).astype(jnp.bfloat16)
    experts = lax.axis_size(("exp", "head"))
    top_count = expert_ids.shape[1]
    capacity = max(2, 2 * tok_dev * top_count // experts)
    flat_ids = expert_ids.reshape(-1)
    onehot = (flat_ids[:, None] == jnp.arange(experts, dtype=jnp.int32)[None, :]).astype(jnp.int32)
    slot_rank = jnp.sum((jnp.cumsum(onehot, axis=0) - onehot) * onehot, axis=1)
    target = (flat_ids * capacity + slot_rank).reshape(tok_dev, top_count)
    slot_ids = jnp.arange(experts * capacity, dtype=jnp.int32)
    route_hits = (target[:, :, None] == slot_ids[None, None, :]).astype(jnp.float32)
    picker = jnp.sum(route_hits, axis=1).astype(jnp.bfloat16)
    dispatched = jnp.einsum(
        "ts,td->sd", picker, normalized, preferred_element_type=jnp.float32
    ).astype(jnp.bfloat16)
    outgoing = dispatched.reshape(experts, capacity, D)
    arrived = lax.all_to_all(outgoing, ("exp", "head"), split_axis=0, concat_axis=0, tiled=True)
    rows_in = arrived.reshape(experts * capacity, D)
    gate_local = w_gate[0]
    up_local = w_up[0]
    down_local = w_down[0]
    shard_rows = lax.all_gather(rows_in, "ctx", axis=0, tiled=True)
    gate_part = jnp.dot(shard_rows, gate_local, preferred_element_type=jnp.float32)
    up_part = jnp.dot(shard_rows, up_local, preferred_element_type=jnp.float32)
    hidden_cols = (jax.nn.silu(gate_part) * up_part).astype(jnp.bfloat16)
    expert_cols = jnp.dot(
        lax.all_gather(hidden_cols, "ctx", axis=1, tiled=True),
        down_local,
        preferred_element_type=jnp.float32,
    ).astype(jnp.bfloat16)
    returned = lax.all_to_all(
        expert_cols.reshape(ctx_count, experts * capacity, down_local.shape[1]),
        "ctx",
        split_axis=0,
        concat_axis=2,
        tiled=True,
    )
    returned_rows = lax.all_to_all(
        returned.reshape(experts, capacity, D),
        ("exp", "head"),
        split_axis=0,
        concat_axis=0,
        tiled=True,
    )
    returned_rows = returned_rows.reshape(experts * capacity, D)
    weighted = jnp.sum(route_hits * route_weights[:, :, None], axis=1)
    moe_sum = jnp.dot(weighted, returned_rows.astype(jnp.float32), precision=lax.Precision.HIGHEST)
    return (residual_sum + moe_sum).astype(jnp.bfloat16)


def solution(mesh):
    placed = (
        P(("groups", "ctx"), None),
        P(("groups", "ctx"), ("exp", "head")),
        P(None, ("exp", "head")),
        P(None, ("exp", "head")),
        P(("exp", "head"), "ctx"),
        P(("groups", "ctx", "exp", "head"), None),
        P(),
        P(("exp", "head"), None, "ctx"),
        P(("exp", "head"), None, "ctx"),
        P(("exp", "head"), None, "ctx"),
        P(("groups", "ctx", "exp", "head"), None),
        P(("groups", "ctx", "exp", "head"), None),
    )
    return jax.shard_map(
        shards,
        mesh=mesh,
        in_specs=placed,
        out_specs=P(("groups", "ctx", "exp", "head"), None),
        check_vma=False,
    )
```

profile of v0, /device:TPU:0, one launch (start us, length us, event | category | flops | bytes accessed | tf_op | source)
XLA Modules:
  0.0 148.8 jit_solution(2626256943590443223)
XLA Ops:
  6.5 0.0 copy-start
  6.5 0.0 copy-start.4
  6.5 0.0 copy-start.5
  6.5 0.0 copy-start.2
  6.5 0.0 copy-start.3
  6.5 0.0 reduce-scatter.4.cloned.1.call-start
  6.6 1.0 reshape.85
  7.6 0.1 iota_compare_fusion
  7.7 15.4 %all_gather.12 = bf16[128,576]{1,0:T(8,128)(2,1)S(1)} all-gather(bf16[32,576]{1,0:T(8,128)(2,1)} %param.12), channel_id=1, replica_groups=mesh['groups'=2,'ctx'=4,'exp'=2,'head'=2] {'ctx'}, dimensions={0}, use_global_device_ids=true | all-gather | bytes 184320 | tf_op jit(solution)/shard_map/all_gather | solution.py:36
  23.1 1.3 fusion.19
  24.4 1.3 fusion.18
  25.7 0.2 convolution_bitcast_fusion.1
  25.8 0.3 select_reduce_fusion
  26.1 0.2 convolution_bitcast_fusion
  26.3 0.3 fusion.23
  26.7 13.5 %all_gather.13 = bf16[128,512]{1,0:T(8,128)(2,1)S(1)} all-gather(bf16[32,512]{1,0:T(8,128)(2,1)S(1)} %bitcast.80), channel_id=1, replica_groups=mesh['groups'=2,'ctx'=4,'exp'=2,'head'=2] {'ctx'}, dimensions={0}, use_global_device_ids=true | all-gather | bytes 163840 | tf_op jit(solution)/shard_map/all_gather | solution.py:72
  40.2 0.0 copy-done
  40.2 0.3 convolution_convert_fusion.1
  40.5 0.1 copy.49
  40.6 0.7 copy.57
  41.3 0.0 reduce-scatter.4.cloned.1.call-update
  41.4 0.0 copy-done.4
  41.4 0.1 copy.45
  41.5 0.1 eq.28
  41.5 0.1 fusion.44
  41.6 0.2 select_reduce_fusion.2
  41.8 0.1 reduce_sum.49
  41.9 0.1 copy.47
  42.0 20.8 %reduce-scatter.4.cloned.1.call-done = bf16[8,3584]{1,0:T(8,128)(2,1)} async-done(((bf16[32,3584]{1,0:T(8,128)(2,1)}), bf16[8,3584]{1,0:T(8,128)(2,1)}) %reduce-scatter.4.cloned.1.call-update) | async-done | bytes 57360
  62.8 0.8 reshape.97
  63.6 0.6 copy.50
  64.3 4.6 %all-to-all-start = ((bf16[4,8,896]{2,1,0:T(8,128)(2,1)}), bf16[4,8,896]{2,1,0:T(8,128)(2,1)S(1)}, u32[]{:S(2)}, u32[]{:S(2)}) async-start(bf16[4,8,896]{2,1,0:T(8,128)(2,1)} %copy.50), calls=%async_computation | async-start | bytes 114688 | tf_op jit(solution)/shard_map/all_to_all | solution.py:78
  68.9 0.0 copy-done.5
  68.9 0.1 convert_reduce_fusion
  68.9 5.6 %all-to-all-done = bf16[4,8,896]{2,1,0:T(8,128)(2,1)S(1)} async-done(((bf16[4,8,896]{2,1,0:T(8,128)(2,1)}), bf16[4,8,896]{2,1,0:T(8,128)(2,1)S(1)}, u32[]{:S(2)}, u32[]{:S(2)}) %all-to-all-start) | async-done | bytes 57376 | tf_op jit(solution)/shard_map/all_to_all | solution.py:78
  74.6 0.0 copy-start.6
  74.6 0.0 copy-done.2
  74.6 0.1 multiply_reduce_fusion
  74.8 0.0 copy-done.3
  74.8 0.3 fusion.1
  75.0 8.2 %all_to_all.34 = bf16[4,8,3584]{2,1,0:T(8,128)(2,1)S(1)} all-to-all(bf16[4,8,3584]{2,1,0:T(8,128)(2,1)S(1)} %fusion.1), channel_id=1, replica_groups=mesh['groups'=2,'ctx'=4,'exp'=2,'head'=2] {'exp','head'}, dimensions={0} | all-to-all | bytes 458752 | tf_op jit(solution)/shard_map/all_to_all | solution.py:99
  83.2 19.1 %all_gather.14 = bf16[128,3584]{1,0:T(8,128)(2,1)S(1)} all-gather(bf16[32,3584]{1,0:T(8,128)(2,1)S(1)} %bitcast.77), channel_id=1, replica_groups=mesh['groups'=2,'ctx'=4,'exp'=2,'head'=2] {'ctx'}, dimensions={0}, use_global_device_ids=true | all-gather | bytes 1146880 | tf_op jit(solution)/shard_map/all_gather | solution.py:104
  102.3 2.7 %fusion.7 = f32[128,512]{1,0:T(8,128)S(1)} fusion(bf16[128,3584]{1,0:T(8,128)(2,1)S(1)} %all_gather.14, bf16[1,3584,512]{2,1,0:T(8,128)(2,1)} %param.19), kind=kOutput, calls=%fused_computation.9 | convolution fusion | flops 469762048 | bytes 4849664 | tf_op jit(solution)/shard_map/dot_general | solution.py:105
  104.9 0.0 copy-done.6
  105.0 0.0 copy-start.1
  105.0 0.6 fusion.15
  105.6 15.8 %all_gather.15 = bf16[128,2048]{1,0:T(8,128)(2,1)S(1)} all-gather(bf16[128,512]{1,0:T(8,128)(2,1)S(1)} %fusion.15), channel_id=1, replica_groups=mesh['groups'=2,'ctx'=4,'exp'=2,'head'=2] {'ctx'}, dimensions={1}, use_global_device_ids=true | all-gather | bytes 655360 | tf_op jit(solution)/shard_map/all_gather | solution.py:109
  121.4 0.0 copy-done.1
  121.4 0.7 fusion.9
  122.1 10.7 %all_to_all.35 = bf16[4,32,896]{2,1,0:T(8,128)(2,1)S(1)} all-to-all(bf16[4,32,896]{2,1,0:T(8,128)(2,1)S(1)} %bitcast.78), channel_id=1, replica_groups=mesh['groups'=2,'ctx'=4,'exp'=2,'head'=2] {'ctx'}, dimensions={0} | all-to-all | bytes 458752 | tf_op jit(solution)/shard_map/all_to_all | solution.py:113
  132.9 0.1 copy.48
  133.0 0.1 reshape.91
  133.1 8.0 %all_to_all.36 = bf16[4,8,3584]{2,1,0:T(8,128)(2,1)S(1)} all-to-all(bf16[4,8,3584]{2,1,0:T(8,128)(2,1)S(1)} %reshape.91), channel_id=1, replica_groups=mesh['groups'=2,'ctx'=4,'exp'=2,'head'=2] {'exp','head'}, dimensions={0} | all-to-all | bytes 458752 | tf_op jit(solution)/shard_map/all_to_all | solution.py:120
  141.1 0.8 fusion.2
  (9 shorter events, 0.1 us)
Async XLA Ops:
  6.5 33.7 %copy-start = (bf16[512,896]{1,0:T(8,128)(2,1)S(1)}, bf16[512,896]{1,0:T(8,128)(2,1)}, u32[]{:S(2)}) copy-start(bf16[512,896]{1,0:T(8,128)(2,1)} %param.16) | copy-start | bytes 2752516
  6.5 34.8 %copy-start.4 = (s32[8,2]{0,1:T(2,128)S(1)}, s32[8,2]{0,1:T(2,128)}, u32[]{:S(2)}) copy-start(s32[8,2]{0,1:T(2,128)} %param.22) | copy-start | bytes 196
  6.5 62.3 %copy-start.5 = (f32[8,2]{0,1:T(2,128)S(1)}, f32[8,2]{0,1:T(2,128)}, u32[]{:S(2)}) copy-start(f32[8,2]{0,1:T(2,128)} %param.23) | copy-start | bytes 196
  6.5 68.1 %copy-start.2 = (bf16[8,3584]{1,0:T(8,128)(2,1)S(1)}, bf16[8,3584]{1,0:T(8,128)(2,1)}, u32[]{:S(2)}) copy-start(bf16[8,3584]{1,0:T(8,128)(2,1)} %param.17) | copy-start | bytes 172036
  6.5 68.2 %copy-start.3 = (f32[3584]{0:T(1024)S(1)}, f32[3584]{0:T(1024)}, u32[]{:S(2)}) copy-start(f32[3584]{0:T(1024)} %param.18) | copy-start | bytes 43012
  6.5 56.2 %reduce-scatter.4.cloned.1.call-start = ((), (), s32[]{:S(2)}) async-start(), calls=%async_computation.5 | async-start | bytes 286720
  64.3 10.3 %all-to-all-start = ((bf16[4,8,896]{2,1,0:T(8,128)(2,1)}), bf16[4,8,896]{2,1,0:T(8,128)(2,1)S(1)}, u32[]{:S(2)}, u32[]{:S(2)}) async-start(bf16[4,8,896]{2,1,0:T(8,128)(2,1)} %copy.50), calls=%async_computation | async-start | bytes 114688 | tf_op jit(solution)/shard_map/all_to_all | solution.py:78
  74.6 30.4 %copy-start.6 = (bf16[1,3584,512]{2,1,0:T(8,128)(2,1)S(1)}, bf16[1,3584,512]{2,1,0:T(8,128)(2,1)}, u32[]{:S(2)}) copy-start(bf16[1,3584,512]{2,1,0:T(8,128)(2,1)} %param.20) | copy-start | bytes 11010052
  105.0 16.4 %copy-start.1 = (bf16[1,2048,896]{2,1,0:T(8,128)(2,1)S(1)}, bf16[1,2048,896]{2,1,0:T(8,128)(2,1)}, u32[]{:S(2)}) copy-start(bf16[1,2048,896]{2,1,0:T(8,128)(2,1)} %param.21) | copy-start | bytes 11010052
Sparse Core Ops, SparseCore 0:
  41.5 21.2 reduce-scatter.3
where the time goes:
time: 149 us
  blocking collectives  90.6 us (61%)
  waiting for transfers between devices  26.4 us (18%)
  between operations  13.6 us (9%)
  matrix products  8.65 us (6%)
  starting transfers between devices  4.63 us (3%)
  local copies, waits for them, and re-layouts  3.88 us (3%)
    unnamed x2, waiting for transfers between devices  20.8 us
    all_gather x1, blocking collectives, shards(): shard_rows = lax.all_gather(rows_in, 'ctx', axis=0, tiled=True)  19.1 us
    all_gather x1, blocking collectives, shards(): lax.all_gather(hidden_cols, 'ctx', axis=1, tiled=True)  15.8 us
    all_gather x1, blocking collectives, shards(): shard_rows = lax.all_gather(latent, 'ctx', axis=0, tiled=True)  15.4 us
    all_gather x1, blocking collectives, shards(): lax.all_gather(attended, 'ctx', axis=0, tiled=True)  13.5 us
    all_to_all x1, blocking collectives, shards(): lax.all_to_all(expert_cols.reshape(ctx_count, experts * capacity, down_lo...  10.7 us
    all_to_all x1, blocking collectives, shards(): lax.all_to_all(outgoing, ('exp', 'head'), split_axis=0, concat_axis=0, ti...  8.16 us
    all_to_all x1, blocking collectives, shards(): lax.all_to_all(returned.reshape(experts, capacity, D), ('exp', 'head'), s...  8.03 us
  transfers between devices with their start and end apart: 2, of which 2 were waited for; matrix products, arithmetic and copies ran while one was open for 0% of the time, Pallas kernels for 0%

commit v1 on v0

--- a/solution.py
+++ b/solution.py
@@ -33,7 +33,12 @@
     query_nope = query_all[:, :, :NOPE]
     query_rope = query_all[:, :, NOPE:]
     query_pos = lax.axis_index("ctx") * qblock + jnp.arange(qblock, dtype=jnp.int32)
-    shard_rows = lax.all_gather(latent, "ctx", axis=0, tiled=True)
+    ring = [latent]
+    for hop in range(3):
+        ring.append(lax.ppermute(ring[-1], "ctx", [(dev, (dev + 1) % 4) for dev in range(4)]))
+    shard_rows = jnp.roll(
+        jnp.concatenate(ring[::-1], axis=0), (lax.axis_index("ctx") + 1) * ring[0].shape[0], axis=0
+    )
     piece_rows = shard_rows.shape[0]
     compressed = shard_rows[:, :LATENT]
     key_nope = (

time: 149 us -> 154 us (1.034)
  blocking collectives: 90.6 us -> 75.1 us
  waiting for transfers between devices: 26.4 us -> 41.4 us
  starting transfers between devices: 4.63 us -> 7.71 us
  local copies, waits for them, and re-layouts: 3.88 us -> 6.03 us
    ppermute x0 -> x3, waiting for transfers between devices: none -> 17.8 us  [shards(): lax.ppermute(ring[-1], 'ctx', [(dev, (dev + 1) % 4) for dev in range(4)])]
    all_gather x1 -> x0, blocking collectives: 15.4 us -> none  [shards(): shard_rows = lax.all_gather(latent, 'ctx', axis=0, tiled=True)]
    ppermute x0 -> x3, starting transfers between devices: none -> 3.11 us  [shards(): lax.ppermute(ring[-1], 'ctx', [(dev, (dev + 1) % 4) for dev in range(4)])]
    unnamed x2, waiting for transfers between devices: 20.8 us -> 17.9 us
    unnamed x19 -> x18, local copies, waits for them, and re-layouts: 2.4 us -> 4.07 us
  transfers between devices with their start and end apart: 2 -> 5, of which waited for: 2 -> 5; matrix products, arithmetic and copies ran while one was open for 0% -> 2% of each run, Pallas kernels for 0% -> 0%
where the time goes in v1:
time: 154 us
  blocking collectives  75.1 us (49%)
  waiting for transfers between devices  41.4 us (27%)
  between operations  13.6 us (9%)
  matrix products  8.93 us (6%)
  starting transfers between devices  7.71 us (5%)
  local copies, waits for them, and re-layouts  6.03 us (4%)
    all_gather x1, blocking collectives, shards(): shard_rows = lax.all_gather(rows_in, 'ctx', axis=0, tiled=True)  19.1 us
    unnamed x2, waiting for transfers between devices  17.9 us
    ppermute x3, waiting for transfers between devices, shards(): lax.ppermute(ring[-1], 'ctx', [(dev, (dev + 1) % 4) for dev in range(4)])  17.8 us
    all_gather x1, blocking collectives, shards(): lax.all_gather(hidden_cols, 'ctx', axis=1, tiled=True)  15.8 us
    all_gather x1, blocking collectives, shards(): lax.all_gather(attended, 'ctx', axis=0, tiled=True)  13.4 us
    all_to_all x1, blocking collectives, shards(): lax.all_to_all(expert_cols.reshape(ctx_count, experts * capacity, down_lo...  10.7 us
    all_to_all x1, blocking collectives, shards(): lax.all_to_all(outgoing, ('exp', 'head'), split_axis=0, concat_axis=0, ti...  8.16 us
    all_to_all x1, blocking collectives, shards(): lax.all_to_all(returned.reshape(experts, capacity, D), ('exp', 'head'), s...  8.03 us
  transfers between devices with their start and end apart: 5, of which 5 were waited for; matrix products, arithmetic and copies ran while one was open for 2% of the time, Pallas kernels for 0%

profile of v1, /device:TPU:0, one launch (start us, length us, event | category | flops | bytes accessed | tf_op | source)
XLA Modules:
  0.0 153.7 jit_solution(5579182870765269741)
XLA Ops:
  6.5 0.0 copy-start
  6.5 0.0 reduce-scatter.4.cloned.1.call-start
  6.5 1.0 copy.45
  7.5 3.1 %collective-permute-start = (bf16[32,576]{0,1:T(8,128)(2,1)S(1)}, bf16[32,576]{0,1:T(8,128)(2,1)S(1)}, u32[]{:S(2)}, u32[]{:S(2)}) collective-permute-start(bf16[32,576]{0,1:T(8,128)(2,1)S(1)} %copy.45), channel_id=1, source_target_pairs={{0,4},{4,8},{8,12},{12,0},{1,5},{5,9},{9,13},{13,1},{2,6},{6,10},{... | collective-permute-start | bytes 110600 | tf_op jit(solution)/shard_map/ppermute | solution.py:38
  10.6 5.9 %collective-permute-done = bf16[32,576]{0,1:T(8,128)(2,1)S(1)} collective-permute-done((bf16[32,576]{0,1:T(8,128)(2,1)S(1)}, bf16[32,576]{0,1:T(8,128)(2,1)S(1)}, u32[]{:S(2)}, u32[]{:S(2)}) %collective-permute-start) | collective-permute-done | bytes 36896 | tf_op jit(solution)/shard_map/ppermute | solution.py:38
  16.5 0.0 collective-permute-start.1
  16.5 6.9 %collective-permute-done.1 = bf16[32,576]{0,1:T(8,128)(2,1)S(1)} collective-permute-done((bf16[32,576]{0,1:T(8,128)(2,1)S(1)}, bf16[32,576]{0,1:T(8,128)(2,1)S(1)}, u32[]{:S(2)}, u32[]{:S(2)}) %collective-permute-start.1) | collective-permute-done | bytes 36896 | tf_op jit(solution)/shard_map/ppermute | solution.py:38
  23.5 0.0 collective-permute-start.2
  23.5 0.1 iota_compare_fusion
  23.5 0.0 copy-start.4
  23.5 0.9 reshape.85
  24.5 0.0 copy-start.2
  24.5 0.8 copy.53
  25.3 0.1 eq.31
  25.4 0.0 copy-start.3
  25.4 5.0 %collective-permute-done.2 = bf16[32,576]{0,1:T(8,128)(2,1)S(1)} collective-permute-done((bf16[32,576]{0,1:T(8,128)(2,1)S(1)}, bf16[32,576]{0,1:T(8,128)(2,1)S(1)}, u32[]{:S(2)}, u32[]{:S(2)}) %collective-permute-start.2) | collective-permute-done | bytes 36896 | tf_op jit(solution)/shard_map/ppermute | solution.py:38
  30.4 0.5 concatenate.6
  30.9 1.4 fusion.19
  32.3 1.4 fusion.18
  33.7 0.2 convolution_bitcast_fusion.2
  33.9 0.3 select_reduce_fusion
  34.2 0.2 convolution_bitcast_fusion
  34.4 0.3 fusion.24
  34.8 13.4 %all_gather.9 = bf16[128,512]{1,0:T(8,128)(2,1)S(1)} all-gather(bf16[32,512]{1,0:T(8,128)(2,1)S(1)} %bitcast.85), channel_id=1, replica_groups=mesh['groups'=2,'ctx'=4,'exp'=2,'head'=2] {'ctx'}, dimensions={0}, use_global_device_ids=true | all-gather | bytes 163840 | tf_op jit(solution)/shard_map/all_gather | solution.py:77
  48.1 0.0 copy-done
  48.2 0.3 convolution_convert_fusion.1
  48.5 0.1 copy.57
  48.6 0.7 copy.64
  49.3 0.0 reduce-scatter.4.cloned.1.call-update
  49.3 0.1 fusion.45
  49.4 0.2 select_reduce_fusion.2
  49.6 0.1 reduce_sum.49
  49.7 0.1 copy.55
  49.8 17.9 %reduce-scatter.4.cloned.1.call-done = bf16[8,3584]{1,0:T(8,128)(2,1)} async-done(((bf16[32,3584]{1,0:T(8,128)(2,1)}), bf16[8,3584]{1,0:T(8,128)(2,1)}) %reduce-scatter.4.cloned.1.call-update) | async-done | bytes 57360
  67.7 0.8 reshape.97
  68.5 0.6 copy.58
  69.1 4.6 %all-to-all-start = ((bf16[4,8,896]{2,1,0:T(8,128)(2,1)}), bf16[4,8,896]{2,1,0:T(8,128)(2,1)S(1)}, u32[]{:S(2)}, u32[]{:S(2)}) async-start(bf16[4,8,896]{2,1,0:T(8,128)(2,1)} %copy.58), calls=%async_computation | async-start | bytes 114688 | tf_op jit(solution)/shard_map/all_to_all | solution.py:83
  73.7 0.0 copy-done.4
  73.7 0.1 convert_reduce_fusion
  73.8 5.6 %all-to-all-done = bf16[4,8,896]{2,1,0:T(8,128)(2,1)S(1)} async-done(((bf16[4,8,896]{2,1,0:T(8,128)(2,1)}), bf16[4,8,896]{2,1,0:T(8,128)(2,1)S(1)}, u32[]{:S(2)}, u32[]{:S(2)}) %all-to-all-start) | async-done | bytes 57376 | tf_op jit(solution)/shard_map/all_to_all | solution.py:83
  79.5 0.0 copy-start.5
  79.5 0.0 copy-done.2
  79.5 0.1 multiply_reduce_fusion
  79.6 0.0 copy-done.3
  79.7 0.3 fusion.1
  79.9 8.2 %all_to_all.34 = bf16[4,8,3584]{2,1,0:T(8,128)(2,1)S(1)} all-to-all(bf16[4,8,3584]{2,1,0:T(8,128)(2,1)S(1)} %fusion.1), channel_id=1, replica_groups=mesh['groups'=2,'ctx'=4,'exp'=2,'head'=2] {'exp','head'}, dimensions={0} | all-to-all | bytes 458752 | tf_op jit(solution)/shard_map/all_to_all | solution.py:104
  88.1 19.1 %all_gather.10 = bf16[128,3584]{1,0:T(8,128)(2,1)S(1)} all-gather(bf16[32,3584]{1,0:T(8,128)(2,1)S(1)} %bitcast.82), channel_id=1, replica_groups=mesh['groups'=2,'ctx'=4,'exp'=2,'head'=2] {'ctx'}, dimensions={0}, use_global_device_ids=true | all-gather | bytes 1146880 | tf_op jit(solution)/shard_map/all_gather | solution.py:109
  107.1 2.7 %fusion.7 = f32[128,512]{1,0:T(8,128)S(1)} fusion(bf16[128,3584]{1,0:T(8,128)(2,1)S(1)} %all_gather.10, bf16[1,3584,512]{2,1,0:T(8,128)(2,1)} %param.19), kind=kOutput, calls=%fused_computation.9 | convolution fusion | flops 469762048 | bytes 4849664 | tf_op jit(solution)/shard_map/dot_general | solution.py:110
  109.8 0.0 copy-done.5
  109.8 0.0 copy-start.1
  109.8 0.7 fusion.15
  110.5 15.8 %all_gather.11 = bf16[128,2048]{1,0:T(8,128)(2,1)S(1)} all-gather(bf16[128,512]{1,0:T(8,128)(2,1)S(1)} %fusion.15), channel_id=1, replica_groups=mesh['groups'=2,'ctx'=4,'exp'=2,'head'=2] {'ctx'}, dimensions={1}, use_global_device_ids=true | all-gather | bytes 655360 | tf_op jit(solution)/shard_map/all_gather | solution.py:114
  126.3 0.0 copy-done.1
  126.3 0.7 fusion.9
  127.0 10.7 %all_to_all.35 = bf16[4,32,896]{2,1,0:T(8,128)(2,1)S(1)} all-to-all(bf16[4,32,896]{2,1,0:T(8,128)(2,1)S(1)} %bitcast.83), channel_id=1, replica_groups=mesh['groups'=2,'ctx'=4,'exp'=2,'head'=2] {'ctx'}, dimensions={0} | all-to-all | bytes 458752 | tf_op jit(solution)/shard_map/all_to_all | solution.py:118
  137.7 0.1 copy.56
  137.9 0.1 reshape.91
  137.9 8.0 %all_to_all.36 = bf16[4,8,3584]{2,1,0:T(8,128)(2,1)S(1)} all-to-all(bf16[4,8,3584]{2,1,0:T(8,128)(2,1)S(1)} %reshape.91), channel_id=1, replica_groups=mesh['groups'=2,'ctx'=4,'exp'=2,'head'=2] {'exp','head'}, dimensions={0} | all-to-all | bytes 458752 | tf_op jit(solution)/shard_map/all_to_all | solution.py:125
  146.0 0.8 fusion.2
  (9 shorter events, 0.1 us)
Async XLA Ops:
  6.5 41.6 %copy-start = (bf16[512,896]{1,0:T(8,128)(2,1)S(1)}, bf16[512,896]{1,0:T(8,128)(2,1)}, u32[]{:S(2)}) copy-start(bf16[512,896]{1,0:T(8,128)(2,1)} %param.16) | copy-start | bytes 2752516
  6.5 61.1 %reduce-scatter.4.cloned.1.call-start = ((), (), s32[]{:S(2)}) async-start(), calls=%async_computation.5 | async-start | bytes 286720
  7.5 9.0 %collective-permute-start = (bf16[32,576]{0,1:T(8,128)(2,1)S(1)}, bf16[32,576]{0,1:T(8,128)(2,1)S(1)}, u32[]{:S(2)}, u32[]{:S(2)}) collective-permute-start(bf16[32,576]{0,1:T(8,128)(2,1)S(1)} %copy.45), channel_id=1, source_target_pairs={{0,4},{4,8},{8,12},{12,0},{1,5},{5,9},{9,13},{13,1},{2,6},{6,10},{... | collective-permute-start | bytes 110600 | tf_op jit(solution)/shard_map/ppermute | solution.py:38
  16.5 6.9 %collective-permute-start.1 = (bf16[32,576]{0,1:T(8,128)(2,1)S(1)}, bf16[32,576]{0,1:T(8,128)(2,1)S(1)}, u32[]{:S(2)}, u32[]{:S(2)}) collective-permute-start(bf16[32,576]{0,1:T(8,128)(2,1)S(1)} %collective-permute-done), channel_id=1, source_target_pairs={{0,4},{4,8},{8,12},{12,0},{1,5},{5,9},{9,13},{13,1},{2,6},{6,10},{... | collective-permute-start | bytes 110600 | tf_op jit(solution)/shard_map/ppermute | solution.py:38
  23.5 6.9 %collective-permute-start.2 = (bf16[32,576]{0,1:T(8,128)(2,1)S(1)}, bf16[32,576]{0,1:T(8,128)(2,1)S(1)}, u32[]{:S(2)}, u32[]{:S(2)}) collective-permute-start(bf16[32,576]{0,1:T(8,128)(2,1)S(1)} %collective-permute-done.1), channel_id=1, source_target_pairs={{0,4},{4,8},{8,12},{12,0},{1,5},{5,9},{9,13},{13,1},{2,6},{6,10},{... | collective-permute-start | bytes 110600 | tf_op jit(solution)/shard_map/ppermute | solution.py:38
  23.5 50.2 %copy-start.4 = (f32[8,2]{0,1:T(2,128)S(1)}, f32[8,2]{0,1:T(2,128)}, u32[]{:S(2)}) copy-start(f32[8,2]{0,1:T(2,128)} %param.23) | copy-start | bytes 196
  24.5 55.0 %copy-start.2 = (bf16[8,3584]{1,0:T(8,128)(2,1)S(1)}, bf16[8,3584]{1,0:T(8,128)(2,1)}, u32[]{:S(2)}) copy-start(bf16[8,3584]{1,0:T(8,128)(2,1)} %param.17) | copy-start | bytes 172036
  25.4 54.3 %copy-start.3 = (f32[3584]{0:T(1024)S(1)}, f32[3584]{0:T(1024)}, u32[]{:S(2)}) copy-start(f32[3584]{0:T(1024)} %param.18) | copy-start | bytes 43012
  69.1 10.3 %all-to-all-start = ((bf16[4,8,896]{2,1,0:T(8,128)(2,1)}), bf16[4,8,896]{2,1,0:T(8,128)(2,1)S(1)}, u32[]{:S(2)}, u32[]{:S(2)}) async-start(bf16[4,8,896]{2,1,0:T(8,128)(2,1)} %copy.58), calls=%async_computation | async-start | bytes 114688 | tf_op jit(solution)/shard_map/all_to_all | solution.py:83
  79.5 30.4 %copy-start.5 = (bf16[1,3584,512]{2,1,0:T(8,128)(2,1)S(1)}, bf16[1,3584,512]{2,1,0:T(8,128)(2,1)}, u32[]{:S(2)}) copy-start(bf16[1,3584,512]{2,1,0:T(8,128)(2,1)} %param.20) | copy-start | bytes 11010052
  109.8 16.4 %copy-start.1 = (bf16[1,2048,896]{2,1,0:T(8,128)(2,1)S(1)}, bf16[1,2048,896]{2,1,0:T(8,128)(2,1)}, u32[]{:S(2)}) copy-start(bf16[1,2048,896]{2,1,0:T(8,128)(2,1)} %param.21) | copy-start | bytes 11010052
Sparse Core Ops, SparseCore 0:
  49.4 18.1 reduce-scatter.3
